TPU v7x, 32 devices: a whole 2x2x4 slice. The times are simulated.
32 devices in a mesh: section: 4 (over y, core), tok: 8 (over z, x).
Axes of the slice: x: 2, y: 2, z: 4, core: 2. Of those that a mesh axis runs over, the one named last changes fastest.
Arguments:
- patches: bfloat16 [1024, 6144], P('tok'), may hold values from -6 to 6
- patch_ids: int32 [1024], P('tok'), may hold values from 0 to 255
- pos_table: bfloat16 [256, 6144], replicated, may hold values from -5 to 5
- token_counts: int32 [8], P('tok'), may hold values from 16 to 128, as said below
- norm_gain: float32 [4, 6144], P('section'), may hold values from 0.25 to 1.75
- norm_bias: float32 [4, 6144], P('section'), may hold values from -3 to 3
- branch_scale: float32 [4, 6144], P('section'), may hold values from 0.5 to 2
- act_range: float32 [4, 6144], P('section'), may hold values from 1 to 8
- weight_range: float32 [4, 6144], P('section'), may hold values from 0.125 to 1
- alpha_index: int32 [4], P('section'), may hold values from 2 to 7
Outputs:
- covariance: float32 [4, 128, 6144], P('section')
- channel_mean: float32 [4, 6144], P('section')
Inputs may be any that keep to these rules, and one draw needn't show every extreme that they name: Each shard's calibration tokens are its first token_counts slots; at least one shard is full in every draw.
All inputs are finite; a program needn't handle non-finite values.
Results may differ from a plain program's by a relative error of at most 0.0067.
Values may be sent and summed in bfloat16 or wider, within the bound.
No kernel may reach another device: no remote copies, remote signals or barrier semaphores. Data moves between devices by JAX's collectives and lax.ppermute only.
A program may use at most 256 MiB of HBM per device.

v0:
```python
import jax
import jax.numpy as jnp
from jax import lax
from jax.sharding import PartitionSpec as P

BLOCK = 128
MICRO = 4


def from_behind(block, axis, distance):
    devices = range(lax.axis_size(axis))
    route = [(i - distance, i) for i in devices if i - distance in devices]
    return lax.ppermute(block, axis, route)


def layer_norm(values, gain, bias_row):
    centre = jnp.mean(values, axis=-1, keepdims=True)
    spread = jnp.mean(jnp.square(values - centre), axis=-1, keepdims=True)
    return (values - centre) * lax.rsqrt(spread + 1e-06) * gain + bias_row


def smoothing(act_row, weight_row, alpha_code):
    exponent = alpha_code.astype(jnp.float32) / 8.0
    return jnp.exp(exponent * jnp.log(act_row) + (exponent - 1.0) * jnp.log(weight_row))


def about_mean(sum_second, sum_first, own_count, mean_row):
    cross = (
        sum_first[:BLOCK][:, None] * mean_row[None, :]
        + mean_row[:BLOCK][:, None] * sum_first[None, :]
    )
    return sum_second - cross + own_count * (mean_row[:BLOCK][:, None] * mean_row[None, :])


def body(
    patches,
    patch_ids,
    pos_table,
    token_counts,
    norm_gain,
    norm_bias,
    branch_scale,
    act_range,
    weight_range,
    alpha_index,
):
    sections = lax.axis_size("section")
    section_index = lax.axis_index("section")
    rows_here = patches.shape[0]
    width = patches.shape[1]
    micro_rows = rows_here // MICRO
    looked_up = jnp.take(pos_table, patch_ids, axis=0).astype(jnp.float32)
    start_rows = (patches.astype(jnp.float32) + looked_up).astype(jnp.bfloat16)
    positions = jnp.arange(rows_here, dtype=jnp.int32)
    valid_flat = (positions < token_counts[0]).astype(jnp.float32)
    factor = smoothing(act_range[0], weight_range[0], alpha_index[0])
    blocks = start_rows.reshape(MICRO, micro_rows, width)
    valid_rows = valid_flat.reshape(MICRO, micro_rows)

    def tick_step(tick, carry):
        incoming, stash = carry
        micro_index = tick - section_index
        active = jnp.logical_and(micro_index >= 0, micro_index < MICRO)
        safe_index = jnp.clip(micro_index, 0, MICRO - 1)
        own_block = lax.dynamic_index_in_dim(blocks, safe_index, 0, keepdims=False)
        current = jnp.where(section_index == 0, own_block, incoming)
        normed = layer_norm(current.astype(jnp.float32), norm_gain[0], norm_bias[0])
        smoothed = (normed / factor).astype(jnp.bfloat16)
        weight_mask = lax.dynamic_index_in_dim(valid_rows, safe_index, 0, keepdims=False).astype(
            jnp.bfloat16
        )
        masked = smoothed * weight_mask[:, None]
        previous = lax.dynamic_index_in_dim(stash, safe_index, 0, keepdims=False)
        kept = jnp.where(active, masked, previous)
        stash = lax.dynamic_update_index_in_dim(stash, kept, safe_index, 0)
        updated = (current.astype(jnp.float32) + branch_scale[0] * jax.nn.gelu(normed)).astype(
            jnp.bfloat16
        )
        passed = from_behind(updated, "section", 1)
        return (passed, stash)

    initial = (
        jnp.zeros((micro_rows, width), jnp.bfloat16),
        jnp.zeros((MICRO, micro_rows, width), jnp.bfloat16),
    )
    carried = lax.fori_loop(0, sections + MICRO - 1, tick_step, initial)
    masked = carried[1].reshape(rows_here, width)
    ones_row = jnp.ones((1, rows_here), jnp.bfloat16)
    sum_first = jnp.dot(ones_row, masked, preferred_element_type=jnp.float32)[0]
    sum_second = lax.dot_general(
        masked[:, :BLOCK], masked, (((0,), (0,)), ((), ())), preferred_element_type=jnp.float32
    )
    own_count = token_counts.astype(jnp.float32)
    total_count, channel_sums = lax.psum((own_count, sum_first), "tok")
    mean_row = channel_sums / total_count
    gram_block = lax.psum(about_mean(sum_second, sum_first, own_count, mean_row), "tok")
    return ((gram_block / total_count)[None], mean_row[None])


def solution(mesh):
    in_specs = (
        P("tok", None),
        P("tok"),
        P(),
        P("tok"),
        P("section", None),
        P("section", None),
        P("section", None),
        P("section", None),
        P("section", None),
        P("section"),
    )
    out_specs = (P("section", None, None), P("section", None))
    return jax.shard_map(body, mesh=mesh, in_specs=in_specs, out_specs=out_specs, check_vma=False)
```

profile of v0, /device:TPU:0, one launch (start us, length us, event | category | flops | bytes accessed | tf_op | source)
XLA Modules:
  0.0 289.3 jit_solution(6521652200142624331)
XLA Ops:
  10.2 2.6 gather_fusion
  13.5 3.6 %add_convert_fusion = bf16[128,6144]{1,0:T(8,128)(2,1)} fusion(bf16[128,6144]{1,0:T(8,128)(2,1)} %param.12, bf16[128,6144]{1,0:T(8,128)(2,1)} %gather_fusion, pred[128]{0:T(512)(128)(4,1)S(1)} %compare_and_fusion), kind=kLoop, calls=%fused_computation.34 | loop fusion | flops 3932160 | bytes 4718720 | tf_op jit(solution)/shard_map/convert_element_type | solution.py:53
  19.2 84.4 %while.16 = (s32[]{:T(128)}, bf16[32,6144]{1,0:T(8,128)(2,1)}, bf16[4,32,6144]{2,1,0:T(8,128)(2,1)}, pred[]{:T(512)}, s32[]{:T(128)}, /*index=5*/bf16[4,32,6144]...) while((s32[]{:T(128)}, bf16[32,6144]{1,0:T(8,128)(2,1)}, ...), condition=%wide.region_3.4_spmd, body=%wide.region_0.3_spmd.sunk | while | flops 6881320 | bytes 6342548 | solution.py:86
  22.1 3.3 %collective-permute-start = (bf16[32,6144]{1,0:T(8,128)(2,1)}, bf16[32,6144]{1,0:T(8,128)(2,1)}, u32[]{:S(2)}, u32[]{:S(2)}) collective-permute-start(bf16[32,6144]{1,0:T(8,128)(2,1)} %fusion.32), channel_id=1, source_target_pairs={{0,8},{8,16},{16,24},{1,9},{9,17},{17,25},{2,10},{10,18},{18,26},{... | collective-permute-start | bytes 1179656 | tf_op jit(solution)/shard_map/while/body/eval_jaxpr/ppermute | solution.py:13
  25.4 1.8 constant_dynamic-slice_fusion.3
  27.1 2.1 bitcast_dynamic-update-slice_fusion.2
  32.1 5.8 %collective-permute-start = (bf16[32,6144]{1,0:T(8,128)(2,1)}, bf16[32,6144]{1,0:T(8,128)(2,1)}, u32[]{:S(2)}, u32[]{:S(2)}) collective-permute-start(bf16[32,6144]{1,0:T(8,128)(2,1)} %fusion.32), channel_id=1, source_target_pairs={{0,8},{8,16},{16,24},{1,9},{9,17},{17,25},{2,10},{10,18},{18,26},{... | collective-permute-start | bytes 1179656 | tf_op jit(solution)/shard_map/while/body/eval_jaxpr/ppermute | solution.py:13
  39.7 2.1 bitcast_dynamic-update-slice_fusion.2
  44.6 5.6 %collective-permute-start = (bf16[32,6144]{1,0:T(8,128)(2,1)}, bf16[32,6144]{1,0:T(8,128)(2,1)}, u32[]{:S(2)}, u32[]{:S(2)}) collective-permute-start(bf16[32,6144]{1,0:T(8,128)(2,1)} %fusion.32), channel_id=1, source_target_pairs={{0,8},{8,16},{16,24},{1,9},{9,17},{17,25},{2,10},{10,18},{18,26},{... | collective-permute-start | bytes 1179656 | tf_op jit(solution)/shard_map/while/body/eval_jaxpr/ppermute | solution.py:13
  52.0 2.1 bitcast_dynamic-update-slice_fusion.2
  57.0 5.7 %collective-permute-start = (bf16[32,6144]{1,0:T(8,128)(2,1)}, bf16[32,6144]{1,0:T(8,128)(2,1)}, u32[]{:S(2)}, u32[]{:S(2)}) collective-permute-start(bf16[32,6144]{1,0:T(8,128)(2,1)} %fusion.32), channel_id=1, source_target_pairs={{0,8},{8,16},{16,24},{1,9},{9,17},{17,25},{2,10},{10,18},{18,26},{... | collective-permute-start | bytes 1179656 | tf_op jit(solution)/shard_map/while/body/eval_jaxpr/ppermute | solution.py:13
  62.6 1.8 constant_dynamic-slice_fusion.3
  64.4 2.1 bitcast_dynamic-update-slice_fusion.2
  69.4 5.6 %collective-permute-start = (bf16[32,6144]{1,0:T(8,128)(2,1)}, bf16[32,6144]{1,0:T(8,128)(2,1)}, u32[]{:S(2)}, u32[]{:S(2)}) collective-permute-start(bf16[32,6144]{1,0:T(8,128)(2,1)} %fusion.32), channel_id=1, source_target_pairs={{0,8},{8,16},{16,24},{1,9},{9,17},{17,25},{2,10},{10,18},{18,26},{... | collective-permute-start | bytes 1179656 | tf_op jit(solution)/shard_map/while/body/eval_jaxpr/ppermute | solution.py:13
  75.0 1.8 constant_dynamic-slice_fusion.3
  76.8 2.1 bitcast_dynamic-update-slice_fusion.2
  81.7 5.6 %collective-permute-start = (bf16[32,6144]{1,0:T(8,128)(2,1)}, bf16[32,6144]{1,0:T(8,128)(2,1)}, u32[]{:S(2)}, u32[]{:S(2)}) collective-permute-start(bf16[32,6144]{1,0:T(8,128)(2,1)} %fusion.32), channel_id=1, source_target_pairs={{0,8},{8,16},{16,24},{1,9},{9,17},{17,25},{2,10},{10,18},{18,26},{... | collective-permute-start | bytes 1179656 | tf_op jit(solution)/shard_map/while/body/eval_jaxpr/ppermute | solution.py:13
  89.2 2.1 bitcast_dynamic-update-slice_fusion.2
  94.1 5.6 %collective-permute-start = (bf16[32,6144]{1,0:T(8,128)(2,1)}, bf16[32,6144]{1,0:T(8,128)(2,1)}, u32[]{:S(2)}, u32[]{:S(2)}) collective-permute-start(bf16[32,6144]{1,0:T(8,128)(2,1)} %fusion.32), channel_id=1, source_target_pairs={{0,8},{8,16},{16,24},{1,9},{9,17},{17,25},{2,10},{10,18},{18,26},{... | collective-permute-start | bytes 1179656 | tf_op jit(solution)/shard_map/while/body/eval_jaxpr/ppermute | solution.py:13
  101.5 2.1 bitcast_dynamic-update-slice_fusion.2
  105.3 37.9 %all-reduce = (f32[6144]{0:T(1024)S(1)}, f32[]{:T(128)}) all-reduce(f32[6144]{0:T(1024)S(1)} %bitcast.49, f32[]{:T(128)} %bitcast.13), channel_id=1, replica_groups=mesh['section'=4,'tok'=8] {'tok'}, use_global_device_ids=true, to_apply=%region_4.5 | all-reduce | flops 6145 | bytes 49160 | tf_op jit(solution)/shard_map/psum | solution.py:94
  143.9 4.2 %fusion.20 = f32[128,6144]{1,0:T(8,128)} fusion(bf16[128,6144]{1,0:T(8,128)(2,1)} %bitcast.40, f32[]{:T(128)} %bitcast.13, f32[6144]{0:T(1024)S(1)} %bitcast.50, f32[128]{0:T(128)S(1)} %slice.18, f32[6144]{0:T(1024)S(1)} %broadcast_divide_fusion, f32[128]{0:T(128)S(1)} %slice.17), kind=kOutput, calls=%fused_computation.32 | convolution fusion | flops 206831616 | bytes 4802048 | tf_op jit(solution)/shard_map/dot_general | solution.py:90
  148.2 129.9 %all-reduce.3.cloned.1.call-done = f32[128,6144]{1,0:T(8,128)} async-done(((f32[128,6144]{1,0:T(8,128)}), f32[128,6144]{1,0:T(8,128)}) %all-reduce.3.cloned.1.call-update) | async-done | bytes 3145744 | tf_op jit(solution)/shard_map/psum | solution.py:96
  278.1 4.4 %divide_bitcast_fusion = f32[1,128,6144]{2,1,0:T(8,128)} fusion(f32[128,6144]{1,0:T(8,128)} %all-reduce.3.cloned.1.call-done, f32[]{:T(128)} %get-tuple-element.240), kind=kLoop, calls=%fused_computation.33 | loop fusion | flops 786432 | bytes 6291460 | tf_op jit(solution)/shard_map/broadcast_in_dim | solution.py:97
  (116 shorter events, 33.7 us)
Async XLA Ops:
  7.2 3.0 %copy-start = (bf16[256,6144]{1,0:T(8,128)(2,1)S(1)}, bf16[256,6144]{1,0:T(8,128)(2,1)}, u32[]{:S(2)}) copy-start(bf16[256,6144]{1,0:T(8,128)(2,1)} %param.14) | copy-start | bytes 9437188
  7.2 270.9 %all-reduce.3.cloned.1.call-start = ((), (), s32[]{:S(2)}) async-start(), calls=%async_computation | async-start | bytes 6291456 | tf_op jit(solution)/shard_map/psum | solution.py:96
  10.1 2.7 copy-start.5
  10.1 2.6 copy-start.6
  19.2 1.6 copy-start.3
  22.1 7.1 %collective-permute-start = (bf16[32,6144]{1,0:T(8,128)(2,1)}, bf16[32,6144]{1,0:T(8,128)(2,1)}, u32[]{:S(2)}, u32[]{:S(2)}) collective-permute-start(bf16[32,6144]{1,0:T(8,128)(2,1)} %fusion.32), channel_id=1, source_target_pairs={{0,8},{8,16},{16,24},{1,9},{9,17},{17,25},{2,10},{10,18},{18,26},{... | collective-permute-start | bytes 1179656 | tf_op jit(solution)/shard_map/while/body/eval_jaxpr/ppermute | solution.py:13
  29.2 1.6 copy-start.2
  29.2 1.6 copy-start.3
  32.1 9.6 %collective-permute-start = (bf16[32,6144]{1,0:T(8,128)(2,1)}, bf16[32,6144]{1,0:T(8,128)(2,1)}, u32[]{:S(2)}, u32[]{:S(2)}) collective-permute-start(bf16[32,6144]{1,0:T(8,128)(2,1)} %fusion.32), channel_id=1, source_target_pairs={{0,8},{8,16},{16,24},{1,9},{9,17},{17,25},{2,10},{10,18},{18,26},{... | collective-permute-start | bytes 1179656 | tf_op jit(solution)/shard_map/while/body/eval_jaxpr/ppermute | solution.py:13
  41.7 1.6 copy-start.2
  41.7 1.6 copy-start.3
  44.6 9.5 %collective-permute-start = (bf16[32,6144]{1,0:T(8,128)(2,1)}, bf16[32,6144]{1,0:T(8,128)(2,1)}, u32[]{:S(2)}, u32[]{:S(2)}) collective-permute-start(bf16[32,6144]{1,0:T(8,128)(2,1)} %fusion.32), channel_id=1, source_target_pairs={{0,8},{8,16},{16,24},{1,9},{9,17},{17,25},{2,10},{10,18},{18,26},{... | collective-permute-start | bytes 1179656 | tf_op jit(solution)/shard_map/while/body/eval_jaxpr/ppermute | solution.py:13
  54.1 1.6 copy-start.2
  54.1 1.6 copy-start.3
  57.0 9.5 %collective-permute-start = (bf16[32,6144]{1,0:T(8,128)(2,1)}, bf16[32,6144]{1,0:T(8,128)(2,1)}, u32[]{:S(2)}, u32[]{:S(2)}) collective-permute-start(bf16[32,6144]{1,0:T(8,128)(2,1)} %fusion.32), channel_id=1, source_target_pairs={{0,8},{8,16},{16,24},{1,9},{9,17},{17,25},{2,10},{10,18},{18,26},{... | collective-permute-start | bytes 1179656 | tf_op jit(solution)/shard_map/while/body/eval_jaxpr/ppermute | solution.py:13
  66.5 1.6 copy-start.2
  66.5 1.6 copy-start.3
  69.4 9.5 %collective-permute-start = (bf16[32,6144]{1,0:T(8,128)(2,1)}, bf16[32,6144]{1,0:T(8,128)(2,1)}, u32[]{:S(2)}, u32[]{:S(2)}) collective-permute-start(bf16[32,6144]{1,0:T(8,128)(2,1)} %fusion.32), channel_id=1, source_target_pairs={{0,8},{8,16},{16,24},{1,9},{9,17},{17,25},{2,10},{10,18},{18,26},{... | collective-permute-start | bytes 1179656 | tf_op jit(solution)/shard_map/while/body/eval_jaxpr/ppermute | solution.py:13
  78.9 1.6 copy-start.2
  78.9 1.6 copy-start.3
  81.7 9.5 %collective-permute-start = (bf16[32,6144]{1,0:T(8,128)(2,1)}, bf16[32,6144]{1,0:T(8,128)(2,1)}, u32[]{:S(2)}, u32[]{:S(2)}) collective-permute-start(bf16[32,6144]{1,0:T(8,128)(2,1)} %fusion.32), channel_id=1, source_target_pairs={{0,8},{8,16},{16,24},{1,9},{9,17},{17,25},{2,10},{10,18},{18,26},{... | collective-permute-start | bytes 1179656 | tf_op jit(solution)/shard_map/while/body/eval_jaxpr/ppermute | solution.py:13
  91.3 1.6 copy-start.3
  94.1 9.5 %collective-permute-start = (bf16[32,6144]{1,0:T(8,128)(2,1)}, bf16[32,6144]{1,0:T(8,128)(2,1)}, u32[]{:S(2)}, u32[]{:S(2)}) collective-permute-start(bf16[32,6144]{1,0:T(8,128)(2,1)} %fusion.32), channel_id=1, source_target_pairs={{0,8},{8,16},{16,24},{1,9},{9,17},{17,25},{2,10},{10,18},{18,26},{... | collective-permute-start | bytes 1179656 | tf_op jit(solution)/shard_map/while/body/eval_jaxpr/ppermute | solution.py:13
  143.9 4.3 %copy-start.4 = (f32[6144]{0:T(1024)}, f32[6144]{0:T(1024)S(1)}, u32[]{:S(2)}) copy-start(f32[6144]{0:T(1024)S(1)} %broadcast_divide_fusion) | copy-start | bytes 73732
  (9 other events, 14.2 us)
Sparse Core Ops, SparseCore 0:
  148.3 129.7 all-reduce.2
where the time goes:
time: 290 us; the launch traced here: 289 us
  waiting for transfers between devices  130 us (45%)
  other arithmetic  45.2 us (16%)
  blocking collectives  37.9 us (13%)
  starting transfers between devices  37.3 us (13%)
  local copies, waits for them, and re-layouts  17.3 us (6%)
  between operations  15.4 us (5%)
  matrix products  5.96 us (2%)
    psum x1, waiting for transfers between devices, body(): lax.psum(about_mean(sum_second, sum_first, own_count, mean_row), 'tok')  130 us
    psum x1, blocking collectives, body(): total_count, channel_sums = lax.psum((own_count, sum_first), 'tok')  37.9 us
    ppermute x7, starting transfers between devices, from_behind(): return lax.ppermute(block, axis, route)  37.3 us
    dynamic_update_slice x7, other arithmetic, tick_step(): stash = lax.dynamic_update_index_in_dim(stash, kept, safe_index, 0)  14.6 us
    dynamic_slice x7, local copies, waits for them, and re-layouts, tick_step(): previous = lax.dynamic_index_in_dim(stash, safe_index, 0, keepdims=False)  12.4 us
    convert_element_type x7, other arithmetic, tick_step(): (current.astype(jnp.float32) + branch_scale[0] * jax.nn.gelu(normed)).ast...  8.82 us
    reduce_sum x7, other arithmetic, layer_norm(): centre = jnp.mean(values, axis=-1, keepdims=True)  8.73 us
  transfers between devices with their start and end apart: 8, of which 1 were waited for; matrix products, arithmetic and copies ran while one was open for 9% of the time, Pallas kernels for 0%

commit v1 on v0

--- a/solution.py
+++ b/solution.py
@@ -93,7 +93,9 @@
     own_count = token_counts.astype(jnp.float32)
     total_count, channel_sums = lax.psum((own_count, sum_first), "tok")
     mean_row = channel_sums / total_count
-    gram_block = lax.psum(about_mean(sum_second, sum_first, own_count, mean_row), "tok")
+    block_2 = about_mean(sum_second, sum_first, own_count, mean_row)
+    terms = lax.all_gather(block_2, "tok")
+    gram_block = jnp.sum(terms, axis=0)
     return ((gram_block / total_count)[None], mean_row[None])
 
 

time: 290 us -> 653 us (2.25)
  waiting for transfers between devices: 130 us -> 482 us
  other arithmetic: 45.2 us -> 56.3 us
    all_gather x0 -> x1, waiting for transfers between devices: none -> 482 us  [body(): terms = lax.all_gather(block_2, 'tok')]
    psum x1 -> x0, waiting for transfers between devices: 130 us -> none  [body(): lax.psum(about_mean(sum_second, sum_first, own_count, mean_row), 'tok')]
    reduce_sum x0 -> x1, other arithmetic: none -> 11 us  [body(): gram_block = jnp.sum(terms, axis=0)]
  transfers between devices with their start and end apart: 8 -> 8, of which waited for: 1 -> 1; matrix products, arithmetic and copies ran while one was open for 9% -> 4% of each run, Pallas kernels for 0% -> 0%
where the time goes in v1:
time: 653 us; the launch traced here: 652 us
  waiting for transfers between devices  482 us (74%)
  other arithmetic  56.3 us (9%)
  blocking collectives  37.9 us (6%)
  starting transfers between devices  37.3 us (6%)
  local copies, waits for them, and re-layouts  17.3 us (3%)
  between operations  15.4 us (2%)
    all_gather x1, waiting for transfers between devices, body(): terms = lax.all_gather(block_2, 'tok')  482 us
    psum x1, blocking collectives, body(): total_count, channel_sums = lax.psum((own_count, sum_first), 'tok')  37.9 us
    ppermute x7, starting transfers between devices, from_behind(): return lax.ppermute(block, axis, route)  37.3 us
    dynamic_update_slice x7, other arithmetic, tick_step(): stash = lax.dynamic_update_index_in_dim(stash, kept, safe_index, 0)  14.6 us
  transfers between devices with their start and end apart: 8, of which 1 were waited for; matrix products, arithmetic and copies ran while one was open for 4% of the time, Pallas kernels for 0%

profile of v1, /device:TPU:0, one launch (start us, length us, event | category | flops | bytes accessed | tf_op | source)
XLA Modules:
  0.0 652.0 jit_solution(14178271756965897950)
XLA Ops:
  10.2 2.6 gather_fusion
  13.5 3.6 add_convert_fusion
  19.2 84.4 %while.16 = (s32[]{:T(128)}, bf16[32,6144]{1,0:T(8,128)(2,1)}, bf16[4,32,6144]{2,1,0:T(8,128)(2,1)}, pred[]{:T(512)}, s32[]{:T(128)}, /*index=5*/bf16[4,32,6144]...) while((s32[]{:T(128)}, bf16[32,6144]{1,0:T(8,128)(2,1)}, ...), condition=%wide.region_3.4_spmd, body=%wide.region_0.3_spmd.sunk | while | flops 6881320 | bytes 6342548 | solution.py:86
  22.1 3.3 collective-permute-start
  25.4 1.8 constant_dynamic-slice_fusion.3
  27.1 2.1 bitcast_dynamic-update-slice_fusion.2
  32.1 5.8 collective-permute-start
  39.7 2.1 bitcast_dynamic-update-slice_fusion.2
  44.6 5.6 collective-permute-start
  52.0 2.1 bitcast_dynamic-update-slice_fusion.2
  57.0 5.7 collective-permute-start
  62.6 1.8 constant_dynamic-slice_fusion.3
  64.4 2.1 bitcast_dynamic-update-slice_fusion.2
  69.4 5.6 collective-permute-start
  76.8 2.1 bitcast_dynamic-update-slice_fusion.2
  81.7 5.6 collective-permute-start
  89.2 2.1 bitcast_dynamic-update-slice_fusion.2
  94.1 5.6 collective-permute-start
  101.5 2.1 bitcast_dynamic-update-slice_fusion.2
  105.3 37.9 %all-reduce = (f32[6144]{0:T(1024)S(1)}, f32[]{:T(128)}) all-reduce(f32[6144]{0:T(1024)S(1)} %bitcast.51, f32[]{:T(128)} %bitcast.13), channel_id=1, replica_groups=mesh['section'=4,'tok'=8] {'tok'}, use_global_device_ids=true, to_apply=%region_4.5 | all-reduce | flops 6145 | bytes 49160 | tf_op jit(solution)/shard_map/psum | solution.py:94
  143.9 4.2 fusion.20
  148.2 481.5 %all-gather.3.cloned.1.call-done = f32[1024,6144]{1,0:T(8,128)} async-done(((f32[128,6144]{1,0:T(8,128)}), f32[1024,6144]{1,0:T(8,128)}) %all-gather.3.cloned.1.call-update) | async-done | bytes 25165840 | tf_op jit(solution)/shard_map/all_gather | solution.py:97
  629.7 11.0 %reduce_sum.37 = f32[128,6144]{1,0:T(8,128)} reduce(f32[8,128,6144]{2,1,0:T(8,128)} %bitcast.40, f32[]{:T(128)} %constant.141.clone.1), dimensions={0}, to_apply=%region_6.7 | reduce | flops 5505024 | bytes 28311556 | tf_op jit(solution)/shard_map/reduce_sum | solution.py:98
  640.7 4.4 divide_bitcast_fusion
  (117 shorter events, 35.5 us)
Async XLA Ops:
  7.2 3.0 copy-start
  7.2 622.5 %all-gather.3.cloned.1.call-start = ((), (), s32[]{:S(2)}) async-start(), calls=%async_computation | async-start | bytes 28311552 | tf_op jit(solution)/shard_map/all_gather | solution.py:97
  10.1 2.7 copy-start.5
  10.1 2.6 copy-start.6
  19.2 1.6 copy-start.3
  22.1 7.1 %collective-permute-start = (bf16[32,6144]{1,0:T(8,128)(2,1)}, bf16[32,6144]{1,0:T(8,128)(2,1)}, u32[]{:S(2)}, u32[]{:S(2)}) collective-permute-start(bf16[32,6144]{1,0:T(8,128)(2,1)} %fusion.32), channel_id=1, source_target_pairs={{0,8},{8,16},{16,24},{1,9},{9,17},{17,25},{2,10},{10,18},{18,26},{... | collective-permute-start | bytes 1179656 | tf_op jit(solution)/shard_map/while/body/eval_jaxpr/ppermute | solution.py:13
  29.2 1.6 copy-start.2
  29.2 1.6 copy-start.3
  32.1 9.6 %collective-permute-start = (bf16[32,6144]{1,0:T(8,128)(2,1)}, bf16[32,6144]{1,0:T(8,128)(2,1)}, u32[]{:S(2)}, u32[]{:S(2)}) collective-permute-start(bf16[32,6144]{1,0:T(8,128)(2,1)} %fusion.32), channel_id=1, source_target_pairs={{0,8},{8,16},{16,24},{1,9},{9,17},{17,25},{2,10},{10,18},{18,26},{... | collective-permute-start | bytes 1179656 | tf_op jit(solution)/shard_map/while/body/eval_jaxpr/ppermute | solution.py:13
  41.7 1.6 copy-start.2
  41.7 1.6 copy-start.3
  44.6 9.5 %collective-permute-start = (bf16[32,6144]{1,0:T(8,128)(2,1)}, bf16[32,6144]{1,0:T(8,128)(2,1)}, u32[]{:S(2)}, u32[]{:S(2)}) collective-permute-start(bf16[32,6144]{1,0:T(8,128)(2,1)} %fusion.32), channel_id=1, source_target_pairs={{0,8},{8,16},{16,24},{1,9},{9,17},{17,25},{2,10},{10,18},{18,26},{... | collective-permute-start | bytes 1179656 | tf_op jit(solution)/shard_map/while/body/eval_jaxpr/ppermute | solution.py:13
  54.1 1.6 copy-start.2
  54.1 1.6 copy-start.3
  57.0 9.5 %collective-permute-start = (bf16[32,6144]{1,0:T(8,128)(2,1)}, bf16[32,6144]{1,0:T(8,128)(2,1)}, u32[]{:S(2)}, u32[]{:S(2)}) collective-permute-start(bf16[32,6144]{1,0:T(8,128)(2,1)} %fusion.32), channel_id=1, source_target_pairs={{0,8},{8,16},{16,24},{1,9},{9,17},{17,25},{2,10},{10,18},{18,26},{... | collective-permute-start | bytes 1179656 | tf_op jit(solution)/shard_map/while/body/eval_jaxpr/ppermute | solution.py:13
  66.5 1.6 copy-start.2
  66.5 1.6 copy-start.3
  69.4 9.5 %collective-permute-start = (bf16[32,6144]{1,0:T(8,128)(2,1)}, bf16[32,6144]{1,0:T(8,128)(2,1)}, u32[]{:S(2)}, u32[]{:S(2)}) collective-permute-start(bf16[32,6144]{1,0:T(8,128)(2,1)} %fusion.32), channel_id=1, source_target_pairs={{0,8},{8,16},{16,24},{1,9},{9,17},{17,25},{2,10},{10,18},{18,26},{... | collective-permute-start | bytes 1179656 | tf_op jit(solution)/shard_map/while/body/eval_jaxpr/ppermute | solution.py:13
  78.9 1.6 copy-start.2
  78.9 1.6 copy-start.3
  81.7 9.5 %collective-permute-start = (bf16[32,6144]{1,0:T(8,128)(2,1)}, bf16[32,6144]{1,0:T(8,128)(2,1)}, u32[]{:S(2)}, u32[]{:S(2)}) collective-permute-start(bf16[32,6144]{1,0:T(8,128)(2,1)} %fusion.32), channel_id=1, source_target_pairs={{0,8},{8,16},{16,24},{1,9},{9,17},{17,25},{2,10},{10,18},{18,26},{... | collective-permute-start | bytes 1179656 | tf_op jit(solution)/shard_map/while/body/eval_jaxpr/ppermute | solution.py:13
  91.3 1.6 copy-start.3
  94.1 9.5 %collective-permute-start = (bf16[32,6144]{1,0:T(8,128)(2,1)}, bf16[32,6144]{1,0:T(8,128)(2,1)}, u32[]{:S(2)}, u32[]{:S(2)}) collective-permute-start(bf16[32,6144]{1,0:T(8,128)(2,1)} %fusion.32), channel_id=1, source_target_pairs={{0,8},{8,16},{16,24},{1,9},{9,17},{17,25},{2,10},{10,18},{18,26},{... | collective-permute-start | bytes 1179656 | tf_op jit(solution)/shard_map/while/body/eval_jaxpr/ppermute | solution.py:13
  143.9 4.3 copy-start.4
  (9 other events, 14.2 us)
Sparse Core Ops, SparseCore 0:
  148.3 481.3 all-gather.2
